TPU v7x, 512 devices: a whole 4x4x16 slice. The times are simulated.
512 devices in a mesh: ctx: 16 (over x, z_hi), mem: 32 (over y, z_lo, core).
Axes of the slice: x: 4, y: 4, z: 16 (z_hi: 4, z_lo: 4; z = z_hi * 4 + z_lo), core: 2. Of those that a mesh axis runs over, the one named last changes fastest.
Arguments:
- queries: bfloat16 [6144, 4096], P('ctx', 'mem'), may hold values from -6 to 6
- keys: bfloat16 [6144, 4096], P('ctx', 'mem'), may hold values from -6 to 6
- values: bfloat16 [6144, 4096], P('ctx', 'mem'), may hold values from -6 to 6
- out_grad: bfloat16 [6144, 4096], P('ctx', 'mem'), may hold values from -6 to 6
- mem_keys: bfloat16 [4096, 4096], P('mem'), may hold values from -6 to 6
- mem_values: bfloat16 [4096, 4096], P('mem'), may hold values from -6 to 6
- gate_logit: float32 [32], P('mem'), may hold values from -3 to 3
- block_ids: int32 [48, 4], P('ctx'), may hold values from 0 to 31, all different within a row
Outputs:
- mixed: bfloat16 [6144, 4096], P('ctx', 'mem')
- query_grad: bfloat16 [6144, 4096], P('ctx', 'mem')
- mem_key_grad: bfloat16 [4096, 4096], P('mem', 'ctx')
- mem_value_grad: bfloat16 [4096, 4096], P('mem', 'ctx')
Inputs may be any that keep to these rules, and one draw needn't show every extreme that they name: `block_ids`: the 4 ids listed for one query block are distinct, and every memory block is listed somewhere.
All inputs are finite; a program needn't handle non-finite values.
Results may differ from a plain program's by a relative error of at most 0.02.
Values may be sent and summed in bfloat16 or wider, within the bound.
No kernel may reach another device: no remote copies, remote signals or barrier semaphores. Data moves between devices by JAX's collectives and lax.ppermute only.
A program may use at most 64 MiB of HBM per device.

v0:
```python
import jax
import jax.numpy as jnp
from jax import lax
from jax.sharding import PartitionSpec as P

HEAD_SIZE = 128
BLOCK = 128


def shards(queries, keys, values, out_grad, mem_keys, mem_values, gate_logit, block_ids):
    tok_count = queries.shape[0]
    columns = queries.shape[1]
    head_count = columns // HEAD_SIZE
    scores_scale_factor = HEAD_SIZE ** (-0.5)
    query_start = lax.axis_index("ctx") * tok_count
    query_heads = queries.reshape(tok_count, head_count, HEAD_SIZE)
    query_pos = query_start + jnp.arange(tok_count, dtype=jnp.int32)
    gate_share = jax.nn.sigmoid(gate_logit)[None, :, None]

    def causal_scores(shard_keys):
        row_count = shard_keys.shape[0]
        scores = (
            jnp.einsum(
                "qhd,khd->hqk",
                query_heads,
                shard_keys.reshape(row_count, head_count, HEAD_SIZE),
                preferred_element_type=jnp.float32,
            )
            * scores_scale_factor
        )
        key_pos = jnp.arange(row_count, dtype=jnp.int32)
        causal = (key_pos[None, :] <= query_pos[:, None])[None]
        return (jnp.where(causal, scores, -1e30), causal)

    run_max = jnp.full((head_count, tok_count), -1e30, jnp.float32)
    shard_keys = lax.all_gather(keys, "ctx", axis=0, tiled=True)
    shard_values = lax.all_gather(values, "ctx", axis=0, tiled=True)
    row_count = shard_keys.shape[0]
    masked, causal = causal_scores(shard_keys)
    new_max = jnp.maximum(run_max, jnp.max(masked, axis=-1))
    weights = jnp.where(causal, jnp.exp(masked - new_max[..., None]), 0.0)
    run_total = jnp.sum(weights, axis=-1)
    run_acc = jnp.einsum(
        "hqk,khd->hqd",
        weights.astype(jnp.bfloat16),
        shard_values.reshape(row_count, head_count, HEAD_SIZE),
        preferred_element_type=jnp.float32,
    )
    run_max, run_total, run_acc = (new_max, run_total, run_acc)
    local_out = (run_acc / run_total[..., None]).transpose(1, 0, 2)
    log_total = run_max + jnp.log(run_total)
    fetched_keys, fetched_values = (
        lax.all_to_all(mem_keys, "mem", split_axis=1, concat_axis=0, tiled=True),
        lax.all_to_all(mem_values, "mem", split_axis=1, concat_axis=0, tiled=True),
    )
    block_count = fetched_keys.shape[0] // BLOCK
    query_block_list = tok_count // BLOCK
    list_len = block_ids.shape[1]
    selected_keys = fetched_keys.reshape(block_count, BLOCK, columns)[block_ids].reshape(
        query_block_list, list_len * BLOCK, head_count, HEAD_SIZE
    )
    selected_values = fetched_values.reshape(block_count, BLOCK, columns)[block_ids].reshape(
        query_block_list, list_len * BLOCK, head_count, HEAD_SIZE
    )
    block_queries = queries.reshape(query_block_list, BLOCK, head_count, HEAD_SIZE)
    memory_score_matrix = (
        jnp.einsum(
            "bqhd,bkhd->bhqk", block_queries, selected_keys, preferred_element_type=jnp.float32
        )
        * scores_scale_factor
    )
    weights = jax.nn.softmax(memory_score_matrix, axis=-1)
    weights_reduced = weights.astype(jnp.bfloat16)
    memory_output = jnp.einsum(
        "bhqk,bkhd->bqhd", weights_reduced, selected_values, preferred_element_type=jnp.float32
    )
    mem_flat = memory_output.reshape(tok_count, head_count, HEAD_SIZE)
    mixed = (
        (gate_share * mem_flat + (1.0 - gate_share) * local_out)
        .reshape(tok_count, columns)
        .astype(jnp.bfloat16)
    )
    grad_full = out_grad.reshape(tok_count, head_count, HEAD_SIZE).astype(jnp.float32)
    grad_mem = gate_share * grad_full
    grad_local = (1.0 - gate_share) * grad_full
    grad_local_low = grad_local.astype(jnp.bfloat16)
    local_delta = jnp.sum(grad_local * local_out, axis=-1).T
    shard_keys = lax.all_gather(keys, "ctx", axis=0, tiled=True)
    shard_values = lax.all_gather(values, "ctx", axis=0, tiled=True)
    row_count = shard_keys.shape[0]
    masked, causal = causal_scores(shard_keys)
    probs = jnp.where(causal, jnp.exp(masked - log_total[..., None]), 0.0)
    grad_probs = jnp.einsum(
        "qhd,khd->hqk",
        grad_local_low,
        shard_values.reshape(row_count, head_count, HEAD_SIZE),
        preferred_element_type=jnp.float32,
    )
    grad_scores = probs * (grad_probs - local_delta[..., None])
    local_grad = (
        jnp.einsum(
            "hqk,khd->qhd",
            grad_scores.astype(jnp.bfloat16),
            shard_keys.reshape(row_count, head_count, HEAD_SIZE),
            preferred_element_type=jnp.float32,
        )
        * scores_scale_factor
    )
    grad_mem_blocks = grad_mem.reshape(query_block_list, BLOCK, head_count, HEAD_SIZE)
    memory_gradient_reduced = grad_mem_blocks.astype(jnp.bfloat16)
    weight_gradient = jnp.einsum(
        "bqhd,bkhd->bhqk",
        memory_gradient_reduced,
        selected_values,
        preferred_element_type=jnp.float32,
    )
    mem_delta = jnp.sum(grad_mem_blocks * memory_output, axis=-1).transpose(0, 2, 1)
    memory_score_gradient = (weights * (weight_gradient - mem_delta[..., None])).astype(
        jnp.bfloat16
    )
    memory_gradient = (
        jnp.einsum(
            "bhqk,bkhd->bqhd",
            memory_score_gradient,
            selected_keys,
            preferred_element_type=jnp.float32,
        )
        * scores_scale_factor
    )
    query_grad = (
        (memory_gradient.reshape(tok_count, head_count, HEAD_SIZE) + local_grad)
        .reshape(tok_count, columns)
        .astype(jnp.bfloat16)
    )
    selected_key_gradient = (
        jnp.einsum(
            "bhqk,bqhd->bkhd",
            memory_score_gradient,
            block_queries,
            preferred_element_type=jnp.float32,
        )
        * scores_scale_factor
    )
    selected_value_gradient = jnp.einsum(
        "bhqk,bqhd->bkhd",
        weights_reduced,
        memory_gradient_reduced,
        preferred_element_type=jnp.float32,
    )
    one_hot = (
        block_ids.reshape(-1)[:, None] == jnp.arange(block_count, dtype=jnp.int32)[None, :]
    ).astype(jnp.float32)
    part_keys = jnp.einsum(
        "jb,jrc->brc",
        one_hot,
        selected_key_gradient.reshape(query_block_list * list_len, BLOCK, columns),
        precision=lax.Precision.HIGHEST,
    ).reshape(block_count * BLOCK, columns)
    part_values = jnp.einsum(
        "jb,jrc->brc",
        one_hot,
        selected_value_gradient.reshape(query_block_list * list_len, BLOCK, columns),
        precision=lax.Precision.HIGHEST,
    ).reshape(block_count * BLOCK, columns)
    keys_low = part_keys.astype(jnp.bfloat16)
    values_low = part_values.astype(jnp.bfloat16)
    owner_keys, owner_values = (
        lax.all_to_all(keys_low, "mem", split_axis=0, concat_axis=1, tiled=True),
        lax.all_to_all(values_low, "mem", split_axis=0, concat_axis=1, tiled=True),
    )
    summed_keys, summed_values = (
        lax.psum_scatter(
            owner_keys.astype(jnp.float32).astype(jnp.bfloat16),
            "ctx",
            scatter_dimension=1,
            tiled=True,
        ).astype(jnp.float32),
        lax.psum_scatter(
            owner_values.astype(jnp.float32).astype(jnp.bfloat16),
            "ctx",
            scatter_dimension=1,
            tiled=True,
        ).astype(jnp.float32),
    )
    return (mixed, query_grad, summed_keys.astype(jnp.bfloat16), summed_values.astype(jnp.bfloat16))


def solution(mesh):
    in_specs = (
        P("ctx", "mem"),
        P("ctx", "mem"),
        P("ctx", "mem"),
        P("ctx", "mem"),
        P("mem", None),
        P("mem", None),
        P("mem"),
        P("ctx", None),
    )
    out_specs = (P("ctx", "mem"), P("ctx", "mem"), P("mem", "ctx"), P("mem", "ctx"))
    return jax.shard_map(shards, mesh=mesh, in_specs=in_specs, out_specs=out_specs, check_vma=False)
```

profile of v0, /device:TPU:8, one launch (start us, length us, event | category | flops | bytes accessed | tf_op | source)
XLA Modules:
  0.0 486.0 jit_solution(12704111752664724385)
XLA Ops:
  7.2 1.7 copy.76
  8.9 1.3 copy.77
  10.2 9.4 %all-to-all-start.1 = ((bf16[128,32,128]{2,0,1:T(8,128)(2,1)}), bf16[128,32,128]{2,0,1:T(8,128)(2,1)S(1)}, u32[]{:S(2)}, u32[]{:S(2)}) async-start(bf16[128,32,128]{2,0,1:T(8,128)(2,1)} %copy.77), calls=%async_computation.1 | async-start | bytes 2097152 | tf_op jit(solution)/shard_map/all_to_all | solution.py:53
  20.4 1.6 copy.74
  22.0 1.4 copy.75
  23.4 21.6 %all-to-all-done.1 = bf16[128,32,128]{2,0,1:T(8,128)(2,1)S(1)} async-done(((bf16[128,32,128]{2,0,1:T(8,128)(2,1)}), bf16[128,32,128]{2,0,1:T(8,128)(2,1)S(1)}, u32[]{:S(2)}, u32[]{:S(2)}) %all-to-all-start.1) | async-done | bytes 1048608 | tf_op jit(solution)/shard_map/all_to_all | solution.py:53
  44.9 6.5 %all-to-all-start = ((bf16[128,32,128]{2,0,1:T(8,128)(2,1)}), bf16[128,32,128]{2,0,1:T(8,128)(2,1)S(1)}, u32[]{:S(2)}, u32[]{:S(2)}) async-start(bf16[128,32,128]{2,0,1:T(8,128)(2,1)} %copy.75), calls=%async_computation | async-start | bytes 2097152 | tf_op jit(solution)/shard_map/all_to_all | solution.py:54
  53.4 51.4 %all-gather.3.cloned.1.call-done = bf16[6144,128]{1,0:T(8,128)(2,1)} async-done(((bf16[384,128]{1,0:T(8,128)(2,1)}), bf16[6144,128]{1,0:T(8,128)(2,1)}) %all-gather.3.cloned.1.call-update) | async-done | bytes 1572880 | tf_op jit(solution)/shard_map/all_gather | solution.py:36
  104.8 3.3 fusion.41
  108.1 3.6 copy-done.1
  111.7 2.3 fusion.1
  115.3 1.3 fusion.42
  116.5 0.8 multiply_reduce_fusion
  117.4 83.4 %all-gather.5.cloned.1.call-done = bf16[6144,128]{1,0:T(8,128)(2,1)} async-done(((bf16[384,128]{1,0:T(8,128)(2,1)}), bf16[6144,128]{1,0:T(8,128)(2,1)}) %all-gather.5.cloned.1.call-update) | async-done | bytes 1572880 | tf_op jit(solution)/shard_map/all_gather | solution.py:37
  200.8 6.4 %fusion.24 = (f32[384]{0:T(512)S(1)}, bf16[384,128]{0,1:T(8,128)(2,1)S(1)}, bf16[384,128]{0,1:T(8,128)(2,1)S(1)}) fusion(bf16[384,128]{0,1:T(8,128)(2,1)S(1)} %copy.80, f32[]{:T(128)} %bitcast.12, f32[384,128]{0,1:T(8,128)S(1)} %copy.79, f32[]{:T(128)} %bitcast, f32[384]{0:T(512)S(1)} %fusion.1, bf16[6144,128]{1,0:T(8,128)(2,1)} %all-gather.5.cloned.1.call-done, ...), kind=kOutput, calls=%fused_computation.38 | convolution fusion | flops 613908096 | bytes 11507720 | tf_op jit(solution)/shard_map/hqk,khd->hqd/dot_general | solution.py:43
  208.2 1.4 convolution_convert_fusion
  209.6 1.5 copy.92
  211.1 5.0 %all-to-all-start.3 = ((bf16[32,128,128]{2,1,0:T(8,128)(2,1)}), bf16[32,128,128]{2,1,0:T(8,128)(2,1)S(1)}, u32[]{:S(2)}, u32[]{:S(2)}) async-start(bf16[32,128,128]{2,1,0:T(8,128)(2,1)} %copy.92), calls=%async_computation.4 | async-start | bytes 2097152 | tf_op jit(solution)/shard_map/all_to_all | solution.py:169
  216.1 1.4 fusion.10
  217.8 1.4 convolution_convert_fusion.1
  219.2 1.4 copy.86
  220.5 20.9 %all-to-all-done.3 = bf16[32,128,128]{2,1,0:T(8,128)(2,1)S(1)} async-done(((bf16[32,128,128]{2,1,0:T(8,128)(2,1)}), bf16[32,128,128]{2,1,0:T(8,128)(2,1)S(1)}, u32[]{:S(2)}, u32[]{:S(2)}) %all-to-all-start.3) | async-done | bytes 1048608 | tf_op jit(solution)/shard_map/all_to_all | solution.py:169
  241.4 6.4 %all-to-all-start.2 = ((bf16[32,128,128]{2,1,0:T(8,128)(2,1)}), bf16[32,128,128]{2,1,0:T(8,128)(2,1)S(1)}, u32[]{:S(2)}, u32[]{:S(2)}) async-start(bf16[32,128,128]{2,1,0:T(8,128)(2,1)} %copy.86), calls=%async_computation.2 | async-start | bytes 2097152 | tf_op jit(solution)/shard_map/all_to_all | solution.py:168
  247.8 1.4 copy.93
  249.3 25.2 %all-to-all-done.2 = bf16[32,128,128]{2,1,0:T(8,128)(2,1)S(1)} async-done(((bf16[32,128,128]{2,1,0:T(8,128)(2,1)}), bf16[32,128,128]{2,1,0:T(8,128)(2,1)S(1)}, u32[]{:S(2)}, u32[]{:S(2)}) %all-to-all-start.2) | async-done | bytes 1048608 | tf_op jit(solution)/shard_map/all_to_all | solution.py:168
  274.5 1.3 copy.87
  275.9 0.8 copy.94
  276.9 8.1 %fusion.15 = bf16[384,128]{1,0:T(8,128)(2,1)} fusion(f32[384,1,128]{2,0,1:T(8,128)S(1)} %bitcast.114, bf16[6144,128]{1,0:T(8,128)(2,1)} %all-gather.3.cloned.1.call-done, f32[384,6144]{1,0:T(8,128)} %copy-done.1, bf16[6144,128]{1,0:T(8,128)(2,1)} %all-gather.5.cloned.1.call-done, f32[384]{0:T(512)S(1)} %get-tuple-element.24, f32[384]{0:T(512)S(1)} %log_add_fusion, ...), kind=kOutput, calls=%fused_computation.28 | convolution fusion | flops 1222410240 | bytes 12980740 | tf_op jit(solution)/shard_map/hqk,khd->qhd/dot_general | solution.py:101
  285.0 79.5 %reduce-scatter.5.cloned.1.call-done = bf16[128,256]{0,1:T(8,128)(2,1)} async-done(((bf16[128,4096]{0,1:T(8,128)(2,1)}), bf16[128,256]{0,1:T(8,128)(2,1)}) %reduce-scatter.5.cloned.1.call-update) | async-done | bytes 65552 | tf_op jit(solution)/shard_map/reduce_scatter | solution.py:178
  364.5 1.6 copy.96
  366.1 111.8 %reduce-scatter.3.cloned.1.call-done = bf16[128,256]{0,1:T(8,128)(2,1)} async-done(((bf16[128,4096]{0,1:T(8,128)(2,1)}), bf16[128,256]{0,1:T(8,128)(2,1)}) %reduce-scatter.3.cloned.1.call-update) | async-done | bytes 65552 | tf_op jit(solution)/shard_map/reduce_scatter | solution.py:172
  477.9 1.6 copy.95
  (34 shorter events, 5.0 us)
Async XLA Ops:
  7.2 97.6 %copy-start = (bf16[384,128]{1,0:T(8,128)(2,1)S(1)}, bf16[384,128]{1,0:T(8,128)(2,1)}, u32[]{:S(2)}) copy-start(bf16[384,128]{1,0:T(8,128)(2,1)} %param.8) | copy-start | bytes 294916
  7.2 45.7 %copy-start.3 = (s32[3,4]{1,0:T(4,128)S(1)}, s32[3,4]{1,0:T(4,128)}, u32[]{:S(2)}) copy-start(s32[3,4]{1,0:T(4,128)} %param.15) | copy-start | bytes 148
  7.2 45.9 %copy-start.2 = (bf16[384,128]{1,0:T(8,128)(2,1)S(1)}, bf16[384,128]{1,0:T(8,128)(2,1)}, u32[]{:S(2)}) copy-start(bf16[384,128]{1,0:T(8,128)(2,1)} %param.11) | copy-start | bytes 294916
  10.2 34.7 %all-to-all-start.1 = ((bf16[128,32,128]{2,0,1:T(8,128)(2,1)}), bf16[128,32,128]{2,0,1:T(8,128)(2,1)S(1)}, u32[]{:S(2)}, u32[]{:S(2)}) async-start(bf16[128,32,128]{2,0,1:T(8,128)(2,1)} %copy.77), calls=%async_computation.1 | async-start | bytes 2097152 | tf_op jit(solution)/shard_map/all_to_all | solution.py:53
  19.6 85.2 %all-gather.3.cloned.1.call-start = ((), (), s32[]{:S(2)}) async-start(), calls=%async_computation.6 | async-start | bytes 1671168 | tf_op jit(solution)/shard_map/all_gather | solution.py:36
  44.9 69.7 %all-to-all-start = ((bf16[128,32,128]{2,0,1:T(8,128)(2,1)}), bf16[128,32,128]{2,0,1:T(8,128)(2,1)S(1)}, u32[]{:S(2)}, u32[]{:S(2)}) async-start(bf16[128,32,128]{2,0,1:T(8,128)(2,1)} %copy.75), calls=%async_computation | async-start | bytes 2097152 | tf_op jit(solution)/shard_map/all_to_all | solution.py:54
  51.4 149.4 %all-gather.5.cloned.1.call-start = ((), (), s32[]{:S(2)}) async-start(), calls=%async_computation.7 | async-start | bytes 1671168 | tf_op jit(solution)/shard_map/all_gather | solution.py:37
  108.1 3.6 copy-start.1
  211.1 30.3 %all-to-all-start.3 = ((bf16[32,128,128]{2,1,0:T(8,128)(2,1)}), bf16[32,128,128]{2,1,0:T(8,128)(2,1)S(1)}, u32[]{:S(2)}, u32[]{:S(2)}) async-start(bf16[32,128,128]{2,1,0:T(8,128)(2,1)} %copy.92), calls=%async_computation.4 | async-start | bytes 2097152 | tf_op jit(solution)/shard_map/all_to_all | solution.py:169
  241.4 33.1 %all-to-all-start.2 = ((bf16[32,128,128]{2,1,0:T(8,128)(2,1)}), bf16[32,128,128]{2,1,0:T(8,128)(2,1)S(1)}, u32[]{:S(2)}, u32[]{:S(2)}) async-start(bf16[32,128,128]{2,1,0:T(8,128)(2,1)} %copy.86), calls=%async_computation.2 | async-start | bytes 2097152 | tf_op jit(solution)/shard_map/all_to_all | solution.py:168
  247.8 116.7 %reduce-scatter.5.cloned.1.call-start = ((), (), s32[]{:S(2)}) async-start(), calls=%async_computation.9 | async-start | bytes 1114112 | tf_op jit(solution)/shard_map/reduce_scatter | solution.py:178
  249.2 228.7 %reduce-scatter.3.cloned.1.call-start = ((), (), s32[]{:S(2)}) async-start(), calls=%async_computation.8 | async-start | bytes 1114112 | tf_op jit(solution)/shard_map/reduce_scatter | solution.py:172
Sparse Core Ops, SparseCore 0:
  23.5 81.2 all-gather.2
  107.8 92.8 all-gather.4
  252.7 111.8 reduce-scatter.4
  368.5 109.4 reduce-scatter.2
where the time goes:
time: 487 us; the launch traced here: 486 us
  waiting for transfers between devices  395 us (81%)
  starting transfers between devices  27.4 us (6%)
  matrix products  25.2 us (5%)
  local copies, waits for them, and re-layouts  21.2 us (4%)
  between operations  14.7 us (3%)
    reduce_scatter x1, waiting for transfers between devices, shards(): lax.psum_scatter(owner_keys.astype(jnp.float32).astype(jnp.bfloat16), 'ct...  112 us
    all_gather x1, waiting for transfers between devices, shards(): shard_values = lax.all_gather(values, 'ctx', axis=0, tiled=True)  83.4 us
    reduce_scatter x1, waiting for transfers between devices, shards(): lax.psum_scatter(owner_values.astype(jnp.float32).astype(jnp.bfloat16), '...  79.5 us
    all_gather x1, waiting for transfers between devices, shards(): shard_keys = lax.all_gather(keys, 'ctx', axis=0, tiled=True)  51.4 us
    all_to_all x1, waiting for transfers between devices, shards(): lax.all_to_all(keys_low, 'mem', split_axis=0, concat_axis=1, tiled=True)  25.2 us
    all_to_all x1, waiting for transfers between devices, shards(): lax.all_to_all(mem_keys, 'mem', split_axis=1, concat_axis=0, tiled=True)  21.6 us
    all_to_all x1, waiting for transfers between devices, shards(): lax.all_to_all(values_low, 'mem', split_axis=0, concat_axis=1, tiled=True)  20.9 us
    unnamed x14, local copies, waits for them, and re-layouts  10.9 us
  transfers between devices with their start and end apart: 8, of which 7 were waited for; matrix products, arithmetic and copies ran while one was open for 6% of the time, Pallas kernels for 0%

commit v1 on v0

v1 whole, which is shorter than its diff:
```python
import jax
import jax.numpy as jnp
from jax import lax
from jax.experimental import pallas as pl
from jax.experimental.pallas import tpu as pltpu
from jax.sharding import Mesh, PartitionSpec as P

HEAD = 128
BLOCK = 128
SEG = 384
QB = 3
LIST = 4
NX = 4
NZ = 4
NBLK = 32
PART = BLOCK // NX
SCALE = HEAD ** -0.5
EXPC = SCALE * 1.4426950408889634
NEG = -1e30
F32 = jnp.float32
BF = jnp.bfloat16
VM = pl.BlockSpec(memory_space=pltpu.VMEM)
SM = pl.BlockSpec(memory_space=pltpu.SMEM)


def nt(a, b):
    return lax.dot_general(a, b, (((1,), (1,)), ((), ())), preferred_element_type=F32)


def nn(a, b):
    return lax.dot_general(a, b, (((1,), (0,)), ((), ())), preferred_element_type=F32)


def tn(a, b):
    return lax.dot_general(a, b, (((0,), (0,)), ((), ())), preferred_element_type=F32)


def split3(row):
    first = row.astype(BF)
    rest = row - first.astype(F32)
    second = rest.astype(BF)
    third = (rest - second.astype(F32)).astype(BF)
    return [first, second, third]


def gathered(mem_ref, ids_ref, block, lo):
    return jnp.concatenate(
        [mem_ref[ids_ref[block, j], lo : lo + PART, :] for j in range(LIST)], axis=0
    )


def mem_forward(ids_ref, gate_ref, qd_ref, mem_ref, e_ref, dw_ref, stat_ref):
    gate = gate_ref[0]
    for block in range(NX * QB):
        seg, b = block // QB, block % QB
        query = qd_ref[seg, b * BLOCK : (b + 1) * BLOCK, :]
        grad = qd_ref[seg, SEG + b * BLOCK : SEG + (b + 1) * BLOCK, :]
        dm = (gate * grad.astype(F32)).astype(BF)
        keys = gathered(mem_ref, ids_ref, block, 0)
        vals = gathered(mem_ref, ids_ref, block, PART)
        scores = nt(keys, query)
        top = jnp.max(scores, axis=0, keepdims=True)
        e = jnp.exp2((scores - top) * EXPC)
        dw = nt(vals, dm)
        e_ref[block] = e
        dw_ref[block] = dw
        stat_ref[0, block : block + 1, :] = top
        stat_ref[1, block : block + 1, :] = jnp.sum(e, axis=0, keepdims=True)
        stat_ref[2, block : block + 1, :] = jnp.sum(e * dw, axis=0, keepdims=True)


def mem_backward(
    ids_ref, gate_ref, pos_ref, qd_ref, mem_ref, e_ref, dw_ref, s0, s1, s2, s3,
    part_ref, o0, o1, o2, o3, grads,
):
    gate = gate_ref[0]
    zh = pos_ref[1]
    grads[...] = jnp.zeros_like(grads)
    stats = (s0, s1, s2, s3)
    top = jnp.maximum(jnp.maximum(s0[0], s1[0]), jnp.maximum(s2[0], s3[0]))
    shares = [jnp.exp2((s[0] - top) * EXPC) for s in stats]
    total = sum(w * s[1] for w, s in zip(shares, stats))
    delta = sum(w * s[2] for w, s in zip(shares, stats)) / total
    factor = shares[0] / total
    for block in range(NX * QB):
        seg, b = block // QB, block % QB
        query = qd_ref[seg, b * BLOCK : (b + 1) * BLOCK, :]
        grad = qd_ref[seg, SEG + b * BLOCK : SEG + (b + 1) * BLOCK, :]
        dm = (gate * grad.astype(F32)).astype(BF)
        keys = gathered(mem_ref, ids_ref, block, 0)
        vals = gathered(mem_ref, ids_ref, block, PART)
        w = e_ref[block] * factor[block : block + 1, :]
        wb = w.astype(BF)
        dmat = (w * (dw_ref[block] - delta[block : block + 1, :])).astype(BF)
        cols = slice(b * BLOCK, (b + 1) * BLOCK)
        part_ref[seg, 0:HEAD, cols] = (gate * tn(vals, wb)).astype(BF)
        part_ref[seg, HEAD : 2 * HEAD, cols] = (SCALE * tn(keys, dmat)).astype(BF)
        dk = nn(dmat, query) * SCALE
        dv = nn(wb, dm)
        for j in range(LIST):
            rows = slice(j * PART, (j + 1) * PART)
            which = ids_ref[block, j]
            grads[which, 0:PART, :] += dk[rows]
            grads[which, PART : 2 * PART, :] += dv[rows]
    for j, out in enumerate((o0, o1, o2, o3)):
        z = lax.rem(zh + j, NZ)
        for y in range(4):
            for core in range(2):
                out[y * 2 + core] = grads[y * 8 + z * 2 + core].astype(BF)


def local_kernel(
    gate_ref, pos_ref, qd_ref, k0, k1, k2, k3, v0, v1, v2, v3, out_ref, s_ref, vk_ref, acc_ref, row_ref
):
    x = pos_ref[0]
    zh = pos_ref[1]
    rest = 1.0 - gate_ref[0]
    keys = (k0, k1, k2, k3)
    vals = (v0, v1, v2, v3)
    for p in range(NZ):
        vk_ref[p, 0:HEAD, :] = vals[p][...].T
        vk_ref[p, HEAD : 2 * HEAD, :] = keys[p][...].T

    @pl.loop(0, NX)
    def _(xp):
        @pl.when(xp < x)
        def _():
            out_ref[xp] = jnp.zeros((3 * HEAD + 16, SEG), BF)
            out_ref[xp, 3 * HEAD : 3 * HEAD + 1, :] = jnp.full((1, SEG), NEG, BF)

        @pl.when(xp >= x)
        def _():
            query = qd_ref[xp, 0:SEG, :]
            grad = qd_ref[xp, SEG : 2 * SEG, :]
            dl = (rest * grad.astype(F32)).astype(BF)
            row_ref[...] = jnp.full((8, SEG), NEG, F32)
            later = xp > x
            for p in range(NZ):
                seg = lax.rem(zh + NZ - p, NZ)

                @pl.when(jnp.logical_or(later, seg <= zh))
                def _():
                    scores = nt(keys[p][...], query)
                    if p == 0:
                        krow = lax.broadcasted_iota(jnp.int32, (SEG, SEG), 0)
                        qcol = lax.broadcasted_iota(jnp.int32, (SEG, SEG), 1)
                        slack = jnp.where(later, SEG, 0)
                        scores = jnp.where(krow <= qcol + slack, scores, NEG)
                    s_ref[p] = scores
                    row_ref[0:1, :] = jnp.maximum(row_ref[0:1, :], jnp.max(scores, axis=0, keepdims=True))

            top = row_ref[0:1, :]
            row_ref[1:3, :] = jnp.zeros((2, SEG), F32)
            acc_ref[...] = jnp.zeros_like(acc_ref)
            for p in range(NZ):
                seg = lax.rem(zh + NZ - p, NZ)

                @pl.when(jnp.logical_or(later, seg <= zh))
                def _():
                    e = jnp.exp2((s_ref[p] - top) * EXPC)
                    ed = e * nt(vals[p][...], dl)
                    row_ref[1:2, :] += jnp.sum(e, axis=0, keepdims=True)
                    row_ref[2:3, :] += jnp.sum(ed, axis=0, keepdims=True)
                    acc_ref[0 : 2 * HEAD, :] += nn(vk_ref[p], e.astype(BF))
                    acc_ref[2 * HEAD : 3 * HEAD, :] += nn(vk_ref[p, HEAD : 2 * HEAD, :], ed.astype(BF))

            out_ref[xp, 0 : 3 * HEAD, :] = acc_ref[...].astype(BF)
            rows = split3(top) + split3(row_ref[1:2, :]) + split3(row_ref[2:3, :])
            rows = [r.astype(F32) for r in rows] + [jnp.zeros((7, SEG), F32)]
            out_ref[xp, 3 * HEAD : 3 * HEAD + 16, :] = jnp.concatenate(rows, axis=0).astype(BF)


def final_kernel(gate_ref, loc_ref, mem_ref, mixed_ref, dq_ref):
    rest = 1.0 - gate_ref[0]

    def stat(i, n):
        rows = loc_ref[i, 3 * HEAD : 3 * HEAD + 16, :].astype(F32)
        return rows[3 * n : 3 * n + 1] + rows[3 * n + 1 : 3 * n + 2] + rows[3 * n + 2 : 3 * n + 3]

    tops = [stat(i, 0) for i in range(NX)]
    top = jnp.maximum(jnp.maximum(tops[0], tops[1]), jnp.maximum(tops[2], tops[3]))
    shares = [jnp.exp2((t - top) * EXPC) for t in tops]
    total = sum(w * stat(i, 1) for i, w in enumerate(shares))
    delta = sum(w * stat(i, 2) for i, w in enumerate(shares)) / total
    factors = [w / total for w in shares]

    def weighted(lo):
        return sum(f * loc_ref[i, lo : lo + HEAD, :].astype(F32) for i, f in enumerate(factors))

    def memory(lo):
        return sum(mem_ref[i, lo : lo + HEAD, :].astype(F32) for i in range(NX))

    mixed = memory(0) + rest * weighted(0)
    dq = memory(HEAD) + SCALE * (weighted(2 * HEAD) - delta * weighted(HEAD))
    mixed_ref[...] = mixed.T.astype(BF)
    dq_ref[...] = dq.T.astype(BF)


def shift(n, by):
    return [(i, (i + by) % n) for i in range(n)]


def shards(queries, keys, values, out_grad, mem_keys, mem_values, gate_logit, block_ids):
    x = lax.axis_index("x")
    zh = lax.axis_index("zh")
    pos = jnp.stack([x, zh]).astype(jnp.int32)
    gate = jax.nn.sigmoid(gate_logit)

    ids_rows = jnp.zeros((16, HEAD), BF).at[0:QB, 0:LIST].set(block_ids.astype(BF))
    packed = jnp.concatenate([queries, out_grad, ids_rows], axis=0)
    qd = lax.all_to_all(jnp.broadcast_to(packed[None], (NX,) + packed.shape), "x", 0, 0)
    ids = qd[:, 2 * SEG : 2 * SEG + QB, 0:LIST].astype(jnp.int32).reshape(NX * QB, LIST)

    mine = jnp.concatenate(
        [
            lax.dynamic_slice_in_dim(mem_keys, x * PART, PART, 0),
            lax.dynamic_slice_in_dim(mem_values, x * PART, PART, 0),
        ],
        axis=0,
    )
    mine = mine.reshape(2 * PART, NBLK, HEAD).transpose(1, 0, 2)
    mem = lax.all_to_all(mine, ("y", "zl", "core"), 0, 0)

    k1 = lax.ppermute(keys, "zh", shift(NZ, 1))
    v3 = lax.ppermute(values, "zh", shift(NZ, -1))
    k3 = lax.ppermute(keys, "zh", shift(NZ, -1))
    v1 = lax.ppermute(values, "zh", shift(NZ, 1))
    k2 = lax.ppermute(k1, "zh", shift(NZ, 1))
    v2 = lax.ppermute(v3, "zh", shift(NZ, -1))

    nq = NX * QB
    e, dw, stat = pl.pallas_call(
        mem_forward,
        out_shape=(
            jax.ShapeDtypeStruct((nq, BLOCK, BLOCK), F32),
            jax.ShapeDtypeStruct((nq, BLOCK, BLOCK), F32),
            jax.ShapeDtypeStruct((3, nq, BLOCK), F32),
        ),
        in_specs=[SM, SM, VM, VM],
        out_specs=(VM, VM, VM),
        name="mem_fwd",
    )(ids, gate, qd, mem)
    others = [lax.ppermute(stat, "x", shift(NX, d)) for d in (1, 2, 3)]

    piece = jax.ShapeDtypeStruct((8, 2 * PART, HEAD), BF)
    part, *pieces = pl.pallas_call(
        mem_backward,
        out_shape=(jax.ShapeDtypeStruct((NX, 2 * HEAD, SEG), BF), piece, piece, piece, piece),
        in_specs=[SM, SM, SM] + [VM] * 8,
        out_specs=(VM,) * 5,
        scratch_shapes=[pltpu.VMEM((NBLK, 2 * PART, HEAD), F32)],
        name="mem_bwd",
    )(ids, gate, pos, qd, mem, e, dw, stat, *others)
    mem_part = lax.all_to_all(part, "x", 0, 0)

    got = [
        lax.ppermute(
            pieces[j],
            ("zh", "zl"),
            [(a * 4 + b, b * 4 + (a + j) % 4) for a in range(4) for b in range(4)],
        )
        for j in range(4)
    ]
    summed = sum(g.astype(F32) for g in got).astype(BF)
    swapped = lax.ppermute(summed, ("x", "y"), [(a * 4 + b, b * 4 + a) for a in range(4) for b in range(4)])
    landed = lax.all_to_all(swapped, ("y", "core"), 0, 0)
    landed = landed.reshape(4, 2, 2, PART, HEAD).transpose(2, 0, 3, 1, 4).reshape(2, BLOCK, 2 * HEAD)

    loc = pl.pallas_call(
        local_kernel,
        out_shape=jax.ShapeDtypeStruct((NX, 3 * HEAD + 16, SEG), BF),
        in_specs=[SM, SM] + [VM] * 9,
        out_specs=VM,
        scratch_shapes=[
            pltpu.VMEM((NZ, SEG, SEG), F32),
            pltpu.VMEM((NZ, 2 * HEAD, SEG), BF),
            pltpu.VMEM((3 * HEAD, SEG), F32),
            pltpu.VMEM((8, SEG), F32),
        ],
        name="local",
    )(gate, pos, qd, keys, k1, k2, k3, values, v1, v2, v3)
    loc_part = lax.all_to_all(loc, "x", 0, 0)

    mixed, dq = pl.pallas_call(
        final_kernel,
        out_shape=(jax.ShapeDtypeStruct((SEG, HEAD), BF),) * 2,
        in_specs=[SM, VM, VM],
        out_specs=(VM, VM),
        name="final",
    )(gate, loc_part, mem_part)
    return mixed, dq, landed[0], landed[1]


def solution(mesh):
    grid = Mesh(mesh.devices.reshape(4, 4, 4, 4, 2), ("x", "zh", "y", "zl", "core"))
    ctx, mem = ("x", "zh"), ("y", "zl", "core")
    in_specs = (P(ctx, mem),) * 4 + (P(mem, None),) * 2 + (P(mem), P(ctx, None))
    out_specs = (P(ctx, mem), P(ctx, mem), P(mem, ctx), P(mem, ctx))
    return jax.shard_map(shards, mesh=grid, in_specs=in_specs, out_specs=out_specs, check_vma=False)
```

time: 487 us -> 197 us (0.40)
  the two profiles are of different devices: /device:TPU:8 before, /device:TPU:64 now
where the time goes in v1:
time: 197 us; the launch traced here: 196 us
  starting transfers between devices  87.6 us (44%)
  waiting for transfers between devices  52.9 us (27%)
  blocking collectives  22.1 us (11%)
  Pallas kernels  21.8 us (11%)
  local copies, waits for them, and re-layouts  6.22 us (3%)
  other arithmetic  3.96 us (2%)
    ppermute x4, starting transfers between devices, shards(): lax.ppermute(pieces[j], ('zh', 'zl'), [(a * 4 + b, b * 4 + (a + j) % 4) f...  24.9 us
    all_to_all x1, blocking collectives, shards(): landed = lax.all_to_all(swapped, ('y', 'core'), 0, 0)  22.1 us
    ppermute x4, waiting for transfers between devices, shards(): lax.ppermute(pieces[j], ('zh', 'zl'), [(a * 4 + b, b * 4 + (a + j) % 4) f...  14.3 us
    pallas_call x1, Pallas kernels, shards(): pl.pallas_call(local_kernel, out_shape=jax.ShapeDtypeStruct((NX, 3 * HEAD...  12.5 us
    ppermute x3, starting transfers between devices, shards(): others = [lax.ppermute(stat, 'x', shift(NX, d)) for d in (1, 2, 3)]  11.8 us
    all_to_all x1, waiting for transfers between devices, shards(): mem_part = lax.all_to_all(part, 'x', 0, 0)  10.9 us
    all_to_all x1, waiting for transfers between devices, shards(): lax.all_to_all(jnp.broadcast_to(packed[None], (NX,) + packed.shape), 'x',...  10.4 us
    ppermute x1, starting transfers between devices, shards(): k1 = lax.ppermute(keys, 'zh', shift(NZ, 1))  9.1 us
  transfers between devices with their start and end apart: 18, of which 11 were waited for; matrix products, arithmetic and copies ran while one was open for 3% of the time, Pallas kernels for 10%

profile of v1, /device:TPU:64, one launch (start us, length us, event | category | flops | bytes accessed | tf_op | source)
XLA Modules:
  0.0 196.2 jit_solution(7100757568185832166)
XLA Ops:
  3.3 4.3 %all-to-all-start = ((bf16[4,784,128]{2,1,0:T(8,128)(2,1)}), bf16[4,784,128]{2,1,0:T(8,128)(2,1)S(1)}, u32[]{:S(2)}, u32[]{:S(2)}) async-start(bf16[4,784,128]{2,1,0:T(8,128)(2,1)} %broadcast_in_dim.2), calls=%async_computation | async-start | bytes 1605632 | tf_op jit(solution)/shard_map/all_to_all | solution.py:211
  7.6 1.1 constant_dynamic-slice_fusion
  9.6 10.4 %all-to-all-done.qd_ref = bf16[4,784,128]{2,1,0:T(8,128)(2,1)S(1)} async-done(((bf16[4,784,128]{2,1,0:T(8,128)(2,1)}), bf16[4,784,128]{2,1,0:T(8,128)(2,1)S(1)}, u32[]{:S(2)}, u32[]{:S(2)}) %all-to-all-start) | async-done | bytes 802848 | tf_op jit(solution)/shard_map/all_to_all | solution.py:211
  20.0 8.3 %all-to-all-start.2 = ((bf16[32,64,128]{2,1,0:T(8,128)(2,1)}), bf16[32,64,128]{2,1,0:T(8,128)(2,1)S(1)}, u32[]{:S(2)}, u32[]{:S(2)}) async-start(bf16[32,64,128]{2,1,0:T(8,128)(2,1)} %bitcast_bitcast_fusion), calls=%async_computation.2 | async-start | bytes 1048576 | tf_op jit(solution)/shard_map/all_to_all | solution.py:222
  28.4 9.1 %collective-permute-start = (bf16[384,128]{1,0:T(8,128)(2,1)S(1)}, bf16[384,128]{1,0:T(8,128)(2,1)S(1)}, u32[]{:S(2)}, u32[]{:S(2)}) collective-permute-start(bf16[384,128]{1,0:T(8,128)(2,1)S(1)} %copy-done.4), channel_id=1, source_target_pairs={{0,32},{32,64},{64,96},{96,0},{1,33},{33,65},{65,97},{97,1},{2,34}... | collective-permute-start | bytes 294920 | tf_op jit(solution)/shard_map/ppermute | solution.py:224
  37.5 2.9 %collective-permute-start.4 = (bf16[384,128]{1,0:T(8,128)(2,1)S(1)}, bf16[384,128]{1,0:T(8,128)(2,1)S(1)}, u32[]{:S(2)}, u32[]{:S(2)}) collective-permute-start(bf16[384,128]{1,0:T(8,128)(2,1)S(1)} %copy-done.5), channel_id=1, source_target_pairs={{0,96},{32,0},{64,32},{96,64},{1,97},{33,1},{65,33},{97,65},{2,98}... | collective-permute-start | bytes 294920 | tf_op jit(solution)/shard_map/ppermute | solution.py:225
  40.4 7.8 %collective-permute-start.2 = (bf16[384,128]{1,0:T(8,128)(2,1)S(1)}, bf16[384,128]{1,0:T(8,128)(2,1)S(1)}, u32[]{:S(2)}, u32[]{:S(2)}) collective-permute-start(bf16[384,128]{1,0:T(8,128)(2,1)S(1)} %copy-done.4), channel_id=1, source_target_pairs={{0,96},{32,0},{64,32},{96,64},{1,97},{33,1},{65,33},{97,65},{2,98}... | collective-permute-start | bytes 294920 | tf_op jit(solution)/shard_map/ppermute | solution.py:226
  48.2 1.9 collective-permute-start.3
  50.9 6.9 %collective-permute-start.1 = (bf16[384,128]{1,0:T(8,128)(2,1)S(1)}, bf16[384,128]{1,0:T(8,128)(2,1)S(1)}, u32[]{:S(2)}, u32[]{:S(2)}) collective-permute-start(bf16[384,128]{1,0:T(8,128)(2,1)S(1)} %collective-permute-done.k1), channel_id=1, source_target_pairs={{0,32},{32,64},{64,96},{96,0},{1,33},{33,65},{65,97},{97,1},{2,34}... | collective-permute-start | bytes 294920 | tf_op jit(solution)/shard_map/ppermute | solution.py:228
  57.8 5.5 %collective-permute-done.4.v3 = bf16[384,128]{1,0:T(8,128)(2,1)S(1)} collective-permute-done((bf16[384,128]{1,0:T(8,128)(2,1)S(1)}, bf16[384,128]{1,0:T(8,128)(2,1)S(1)}, u32[]{:S(2)}, u32[]{:S(2)}) %collective-permute-start.4) | collective-permute-done | bytes 98336 | tf_op jit(solution)/shard_map/ppermute | solution.py:225
  63.3 1.9 collective-permute-start.5
  65.8 2.5 %collective-permute-done.1.k2 = bf16[384,128]{1,0:T(8,128)(2,1)S(1)} collective-permute-done((bf16[384,128]{1,0:T(8,128)(2,1)S(1)}, bf16[384,128]{1,0:T(8,128)(2,1)S(1)}, u32[]{:S(2)}, u32[]{:S(2)}) %collective-permute-start.1) | collective-permute-done | bytes 98336 | tf_op jit(solution)/shard_map/ppermute | solution.py:228
  68.3 6.7 %collective-permute-done.5.v2 = bf16[384,128]{1,0:T(8,128)(2,1)S(1)} collective-permute-done((bf16[384,128]{1,0:T(8,128)(2,1)S(1)}, bf16[384,128]{1,0:T(8,128)(2,1)S(1)}, u32[]{:S(2)}, u32[]{:S(2)}) %collective-permute-start.5) | collective-permute-done | bytes 98336 | tf_op jit(solution)/shard_map/ppermute | solution.py:229
  75.8 12.5 %local.1 = bf16[4,400,384]{2,1,0:T(8,128)(2,1)} custom-call(f32[1]{0:T(128)S(6)} %div.3.gate_ref, s32[2]{0:T(128)} %pad_add_fusion.pos_ref, bf16[4,784,128]{2,1,0:T(8,128)(2,1)} %copy-done, bf16[384,128]{1,0:T(8,128)(2,1)} %k0.1, bf16[384,128]{1,0:T(8,128)(2,1)} %copy-done.6, bf16[384,128]{1,0:T(8,128)(2,1)} %copy-done.10, bf16[384,128]{1,0:T(8,128)(2,1)} %copy-done.8, ...), custom_call_target="tpu_custom_call" | custom-call | tf_op jit(solution)/shard_map/local/pallas_call | solution.py:269
  88.2 3.5 %all-to-all-start.1 = ((bf16[4,400,384]{2,1,0:T(8,128)(2,1)}), bf16[4,400,384]{2,1,0:T(8,128)(2,1)S(1)}, u32[]{:S(2)}, u32[]{:S(2)}) async-start(bf16[4,400,384]{2,1,0:T(8,128)(2,1)} %local.1), calls=%async_computation.1 | async-start | bytes 2457600 | tf_op jit(solution)/shard_map/all_to_all | solution.py:282
  93.1 3.1 %mem_fwd.1 = (f32[12,128,128]{2,1,0:T(8,128)}, f32[12,128,128]{2,1,0:T(8,128)}, f32[3,12,128]{2,1,0:T(8,128)}) custom-call(s32[12,4]{1,0:T(8,128)} %reshape.62.ids_ref, f32[1]{0:T(128)S(6)} %div.3.gate_ref, bf16[4,784,128]{2,1,0:T(8,128)(2,1)} %copy-done, bf16[32,64,128]{2,1,0:T(8,128)(2,1)} %copy-done.2), custom_call_target="tpu_custom_call" | custom-call | tf_op jit(solution)/shard_map/mem_fwd/pallas_call | solution.py:232
  96.2 3.9 %collective-permute-start.6 = (f32[3,12,128]{2,1,0:T(8,128)}, f32[3,12,128]{2,1,0:T(8,128)S(1)}, u32[]{:S(2)}, u32[]{:S(2)}) collective-permute-start(f32[3,12,128]{2,1,0:T(8,128)} %get-tuple-element.28.s0), channel_id=1, source_target_pairs={{0,128},{128,256},{256,384},{384,0},{1,129},{129,257},{257,385},{3... | collective-permute-start | bytes 55304 | tf_op jit(solution)/shard_map/ppermute | solution.py:243
  100.1 4.6 %collective-permute-start.7 = (f32[3,12,128]{2,1,0:T(8,128)}, f32[3,12,128]{2,1,0:T(8,128)S(1)}, u32[]{:S(2)}, u32[]{:S(2)}) collective-permute-start(f32[3,12,128]{2,1,0:T(8,128)} %get-tuple-element.28.s0), channel_id=1, source_target_pairs={{0,256},{128,384},{256,0},{384,128},{1,257},{129,385},{257,1},{385... | collective-permute-start | bytes 55304 | tf_op jit(solution)/shard_map/ppermute | solution.py:243
  104.7 3.4 %collective-permute-start.8 = (f32[3,12,128]{2,1,0:T(8,128)}, f32[3,12,128]{2,1,0:T(8,128)S(1)}, u32[]{:S(2)}, u32[]{:S(2)}) collective-permute-start(f32[3,12,128]{2,1,0:T(8,128)} %get-tuple-element.28.s0), channel_id=1, source_target_pairs={{0,384},{128,0},{256,128},{384,256},{1,385},{129,1},{257,129},{385... | collective-permute-start | bytes 55304 | tf_op jit(solution)/shard_map/ppermute | solution.py:243
  108.6 1.7 collective-permute-done.7.s2
  111.2 3.6 %mem_bwd.1 = (bf16[4,256,384]{2,1,0:T(8,128)(2,1)}, bf16[8,64,128]{2,1,0:T(8,128)(2,1)}, bf16[8,64,128]{2,1,0:T(8,128)(2,1)}, bf16[8,64,128]{2,1,0:T(8,128)(2,1)}, bf16[8,64,128]{2,1,0:T(8,128)(2,1)}) custom-call(s32[12,4]{1,0:T(8,128)} %reshape.62.ids_ref, f32[1]{0:T(128)S(6)} %div.3.gate_ref, s32[2]{0:T(128)} %pad_add_fusion.pos_ref, ...), custom_call_target="tpu_custom_call" | custom-call | tf_op jit(solution)/shard_map/mem_bwd/pallas_call | solution.py:246
  114.8 9.2 %collective-permute-start.10 = (bf16[8,64,128]{2,1,0:T(8,128)(2,1)}, bf16[8,64,128]{2,1,0:T(8,128)(2,1)S(1)}, u32[]{:S(2)}, u32[]{:S(2)}) collective-permute-start(bf16[8,64,128]{2,1,0:T(8,128)(2,1)} %get-tuple-element.33), channel_id=1, source_target_pairs={{0,2},{2,34},{4,66},{6,98},{32,4},{34,36},{36,68},{38,100},{64,6},... | collective-permute-start | bytes 393224 | tf_op jit(solution)/shard_map/ppermute | solution.py:257
  124.0 1.9 collective-permute-start.11
  125.9 3.8 %collective-permute-start.12 = (bf16[8,64,128]{2,1,0:T(8,128)(2,1)}, bf16[8,64,128]{2,1,0:T(8,128)(2,1)S(1)}, u32[]{:S(2)}, u32[]{:S(2)}) collective-permute-start(bf16[8,64,128]{2,1,0:T(8,128)(2,1)} %get-tuple-element.35), channel_id=1, source_target_pairs={{0,6},{2,38},{4,70},{6,102},{32,0},{34,32},{36,64},{38,96},{64,2},... | collective-permute-start | bytes 393224 | tf_op jit(solution)/shard_map/ppermute | solution.py:257
  129.8 10.0 %collective-permute-start.9 = (bf16[8,64,128]{2,1,0:T(8,128)(2,1)}, bf16[8,64,128]{2,1,0:T(8,128)(2,1)S(1)}, u32[]{:S(2)}, u32[]{:S(2)}) collective-permute-start(bf16[8,64,128]{2,1,0:T(8,128)(2,1)} %get-tuple-element.32), channel_id=1, source_target_pairs={{0,0},{2,32},{4,64},{6,96},{32,2},{34,34},{36,66},{38,98},{64,4},{... | collective-permute-start | bytes 393224 | tf_op jit(solution)/shard_map/ppermute | solution.py:257
  139.7 3.8 %collective-permute-done.11 = bf16[8,64,128]{2,1,0:T(8,128)(2,1)S(1)} collective-permute-done((bf16[8,64,128]{2,1,0:T(8,128)(2,1)}, bf16[8,64,128]{2,1,0:T(8,128)(2,1)S(1)}, u32[]{:S(2)}, u32[]{:S(2)}) %collective-permute-start.11) | collective-permute-done | bytes 131104 | tf_op jit(solution)/shard_map/ppermute | solution.py:257
  143.5 4.8 %collective-permute-done.12 = bf16[8,64,128]{2,1,0:T(8,128)(2,1)S(1)} collective-permute-done((bf16[8,64,128]{2,1,0:T(8,128)(2,1)}, bf16[8,64,128]{2,1,0:T(8,128)(2,1)S(1)}, u32[]{:S(2)}, u32[]{:S(2)}) %collective-permute-start.12) | collective-permute-done | bytes 131104 | tf_op jit(solution)/shard_map/ppermute | solution.py:257
  148.3 5.7 %collective-permute-done.9 = bf16[8,64,128]{2,1,0:T(8,128)(2,1)S(1)} collective-permute-done((bf16[8,64,128]{2,1,0:T(8,128)(2,1)}, bf16[8,64,128]{2,1,0:T(8,128)(2,1)S(1)}, u32[]{:S(2)}, u32[]{:S(2)}) %collective-permute-start.9) | collective-permute-done | bytes 131104 | tf_op jit(solution)/shard_map/ppermute | solution.py:257
  154.8 22.1 %all_to_all.25 = bf16[8,64,128]{2,1,0:T(8,128)(2,1)S(1)} all-to-all(bf16[8,64,128]{2,1,0:T(8,128)(2,1)S(1)} %collective-permute-done.13), channel_id=1, replica_groups=mesh['x'=4,'zh'=4,'y'=4,'zl'=4,'core'=2] {'y','core'}, dimensions={0} | all-to-all | bytes 262144 | tf_op jit(solution)/shard_map/all_to_all | solution.py:266
  176.9 3.5 %all-to-all-start.3 = ((bf16[4,256,384]{2,1,0:T(8,128)(2,1)}), bf16[4,256,384]{2,1,0:T(8,128)(2,1)S(1)}, u32[]{:S(2)}, u32[]{:S(2)}) async-start(bf16[4,256,384]{2,1,0:T(8,128)(2,1)} %get-tuple-element.29), calls=%async_computation.3 | async-start | bytes 1572864 | tf_op jit(solution)/shard_map/all_to_all | solution.py:254
  181.8 10.9 %all-to-all-done.3.mem_ref = bf16[4,256,384]{2,1,0:T(8,128)(2,1)S(1)} async-done(((bf16[4,256,384]{2,1,0:T(8,128)(2,1)}), bf16[4,256,384]{2,1,0:T(8,128)(2,1)S(1)}, u32[]{:S(2)}, u32[]{:S(2)}) %all-to-all-start.3) | async-done | bytes 786464 | tf_op jit(solution)/shard_map/all_to_all | solution.py:254
  193.6 2.6 %final.1 = (bf16[384,128]{1,0:T(8,128)(2,1)}, bf16[384,128]{1,0:T(8,128)(2,1)}) custom-call(f32[1]{0:T(128)S(6)} %div.3.gate_ref, bf16[4,400,384]{2,1,0:T(8,128)(2,1)} %copy-done.1, bf16[4,256,384]{2,1,0:T(8,128)(2,1)} %copy-done.3), custom_call_target="tpu_custom_call" | custom-call | tf_op jit(solution)/shard_map/final/pallas_call | solution.py:284
  (53 shorter events, 10.7 us)
Async XLA Ops:
  3.3 16.8 %all-to-all-start = ((bf16[4,784,128]{2,1,0:T(8,128)(2,1)}), bf16[4,784,128]{2,1,0:T(8,128)(2,1)S(1)}, u32[]{:S(2)}, u32[]{:S(2)}) async-start(bf16[4,784,128]{2,1,0:T(8,128)(2,1)} %broadcast_in_dim.2), calls=%async_computation | async-start | bytes 1605632 | tf_op jit(solution)/shard_map/all_to_all | solution.py:211
  8.6 19.7 %copy-start.4 = (bf16[384,128]{1,0:T(8,128)(2,1)S(1)}, bf16[384,128]{1,0:T(8,128)(2,1)}, u32[]{:S(2)}) copy-start(bf16[384,128]{1,0:T(8,128)(2,1)} %k0.1) | copy-start | bytes 294916
  8.7 28.9 %copy-start.5 = (bf16[384,128]{1,0:T(8,128)(2,1)S(1)}, bf16[384,128]{1,0:T(8,128)(2,1)}, u32[]{:S(2)}) copy-start(bf16[384,128]{1,0:T(8,128)(2,1)} %v0.1) | copy-start | bytes 294916
  20.0 55.0 %copy-start = (bf16[4,784,128]{2,1,0:T(8,128)(2,1)}, bf16[4,784,128]{2,1,0:T(8,128)(2,1)S(1)}, u32[]{:S(2)}) copy-start(bf16[4,784,128]{2,1,0:T(8,128)(2,1)S(1)} %all-to-all-done.qd_ref) | copy-start | bytes 2408452
  20.0 68.2 %all-to-all-start.2 = ((bf16[32,64,128]{2,1,0:T(8,128)(2,1)}), bf16[32,64,128]{2,1,0:T(8,128)(2,1)S(1)}, u32[]{:S(2)}, u32[]{:S(2)}) async-start(bf16[32,64,128]{2,1,0:T(8,128)(2,1)} %bitcast_bitcast_fusion), calls=%async_computation.2 | async-start | bytes 1048576 | tf_op jit(solution)/shard_map/all_to_all | solution.py:222
  28.4 22.5 %collective-permute-start = (bf16[384,128]{1,0:T(8,128)(2,1)S(1)}, bf16[384,128]{1,0:T(8,128)(2,1)S(1)}, u32[]{:S(2)}, u32[]{:S(2)}) collective-permute-start(bf16[384,128]{1,0:T(8,128)(2,1)S(1)} %copy-done.4), channel_id=1, source_target_pairs={{0,32},{32,64},{64,96},{96,0},{1,33},{33,65},{65,97},{97,1},{2,34}... | collective-permute-start | bytes 294920 | tf_op jit(solution)/shard_map/ppermute | solution.py:224
  37.5 25.8 %collective-permute-start.4 = (bf16[384,128]{1,0:T(8,128)(2,1)S(1)}, bf16[384,128]{1,0:T(8,128)(2,1)S(1)}, u32[]{:S(2)}, u32[]{:S(2)}) collective-permute-start(bf16[384,128]{1,0:T(8,128)(2,1)S(1)} %copy-done.5), channel_id=1, source_target_pairs={{0,96},{32,0},{64,32},{96,64},{1,97},{33,1},{65,33},{97,65},{2,98}... | collective-permute-start | bytes 294920 | tf_op jit(solution)/shard_map/ppermute | solution.py:225
  40.4 25.4 %collective-permute-start.2 = (bf16[384,128]{1,0:T(8,128)(2,1)S(1)}, bf16[384,128]{1,0:T(8,128)(2,1)S(1)}, u32[]{:S(2)}, u32[]{:S(2)}) collective-permute-start(bf16[384,128]{1,0:T(8,128)(2,1)S(1)} %copy-done.4), channel_id=1, source_target_pairs={{0,96},{32,0},{64,32},{96,64},{1,97},{33,1},{65,33},{97,65},{2,98}... | collective-permute-start | bytes 294920 | tf_op jit(solution)/shard_map/ppermute | solution.py:226
  48.2 17.6 %collective-permute-start.3 = (bf16[384,128]{1,0:T(8,128)(2,1)S(1)}, bf16[384,128]{1,0:T(8,128)(2,1)S(1)}, u32[]{:S(2)}, u32[]{:S(2)}) collective-permute-start(bf16[384,128]{1,0:T(8,128)(2,1)S(1)} %copy-done.5), channel_id=1, source_target_pairs={{0,32},{32,64},{64,96},{96,0},{1,33},{33,65},{65,97},{97,1},{2,34}... | collective-permute-start | bytes 294920 | tf_op jit(solution)/shard_map/ppermute | solution.py:227
  50.9 24.2 %copy-start.6 = (bf16[384,128]{1,0:T(8,128)(2,1)}, bf16[384,128]{1,0:T(8,128)(2,1)S(1)}, u32[]{:S(2)}) copy-start(bf16[384,128]{1,0:T(8,128)(2,1)S(1)} %collective-permute-done.k1) | copy-start | bytes 294916
  50.9 17.4 %collective-permute-start.1 = (bf16[384,128]{1,0:T(8,128)(2,1)S(1)}, bf16[384,128]{1,0:T(8,128)(2,1)S(1)}, u32[]{:S(2)}, u32[]{:S(2)}) collective-permute-start(bf16[384,128]{1,0:T(8,128)(2,1)S(1)} %collective-permute-done.k1), channel_id=1, source_target_pairs={{0,32},{32,64},{64,96},{96,0},{1,33},{33,65},{65,97},{97,1},{2,34}... | collective-permute-start | bytes 294920 | tf_op jit(solution)/shard_map/ppermute | solution.py:228
  63.3 11.8 %copy-start.7 = (bf16[384,128]{1,0:T(8,128)(2,1)}, bf16[384,128]{1,0:T(8,128)(2,1)S(1)}, u32[]{:S(2)}) copy-start(bf16[384,128]{1,0:T(8,128)(2,1)S(1)} %collective-permute-done.4.v3) | copy-start | bytes 294916
  63.3 11.8 %collective-permute-start.5 = (bf16[384,128]{1,0:T(8,128)(2,1)S(1)}, bf16[384,128]{1,0:T(8,128)(2,1)S(1)}, u32[]{:S(2)}, u32[]{:S(2)}) collective-permute-start(bf16[384,128]{1,0:T(8,128)(2,1)S(1)} %collective-permute-done.4.v3), channel_id=1, source_target_pairs={{0,96},{32,0},{64,32},{96,64},{1,97},{33,1},{65,33},{97,65},{2,98}... | collective-permute-start | bytes 294920 | tf_op jit(solution)/shard_map/ppermute | solution.py:229
  65.8 9.3 %copy-start.8 = (bf16[384,128]{1,0:T(8,128)(2,1)}, bf16[384,128]{1,0:T(8,128)(2,1)S(1)}, u32[]{:S(2)}) copy-start(bf16[384,128]{1,0:T(8,128)(2,1)S(1)} %collective-permute-done.2.k3) | copy-start | bytes 294916
  65.8 9.3 %copy-start.9 = (bf16[384,128]{1,0:T(8,128)(2,1)}, bf16[384,128]{1,0:T(8,128)(2,1)S(1)}, u32[]{:S(2)}) copy-start(bf16[384,128]{1,0:T(8,128)(2,1)S(1)} %collective-permute-done.3.v1) | copy-start | bytes 294916
  68.3 6.8 %copy-start.10 = (bf16[384,128]{1,0:T(8,128)(2,1)}, bf16[384,128]{1,0:T(8,128)(2,1)S(1)}, u32[]{:S(2)}) copy-start(bf16[384,128]{1,0:T(8,128)(2,1)S(1)} %collective-permute-done.1.k2) | copy-start | bytes 294916
  75.1 0.6 copy-start.11
  88.2 4.3 %copy-start.2 = (bf16[32,64,128]{2,1,0:T(8,128)(2,1)}, bf16[32,64,128]{2,1,0:T(8,128)(2,1)S(1)}, u32[]{:S(2)}) copy-start(bf16[32,64,128]{2,1,0:T(8,128)(2,1)S(1)} %all-to-all-done.2.mem_ref) | copy-start | bytes 1572868
  88.2 66.6 %all-to-all-start.1 = ((bf16[4,400,384]{2,1,0:T(8,128)(2,1)}), bf16[4,400,384]{2,1,0:T(8,128)(2,1)S(1)}, u32[]{:S(2)}, u32[]{:S(2)}) async-start(bf16[4,400,384]{2,1,0:T(8,128)(2,1)} %local.1), calls=%async_computation.1 | async-start | bytes 2457600 | tf_op jit(solution)/shard_map/all_to_all | solution.py:282
  96.2 12.4 %collective-permute-start.6 = (f32[3,12,128]{2,1,0:T(8,128)}, f32[3,12,128]{2,1,0:T(8,128)S(1)}, u32[]{:S(2)}, u32[]{:S(2)}) collective-permute-start(f32[3,12,128]{2,1,0:T(8,128)} %get-tuple-element.28.s0), channel_id=1, source_target_pairs={{0,128},{128,256},{256,384},{384,0},{1,129},{129,257},{257,385},{3... | collective-permute-start | bytes 55304 | tf_op jit(solution)/shard_map/ppermute | solution.py:243
  100.1 10.2 %collective-permute-start.7 = (f32[3,12,128]{2,1,0:T(8,128)}, f32[3,12,128]{2,1,0:T(8,128)S(1)}, u32[]{:S(2)}, u32[]{:S(2)}) collective-permute-start(f32[3,12,128]{2,1,0:T(8,128)} %get-tuple-element.28.s0), channel_id=1, source_target_pairs={{0,256},{128,384},{256,0},{384,128},{1,257},{129,385},{257,1},{385... | collective-permute-start | bytes 55304 | tf_op jit(solution)/shard_map/ppermute | solution.py:243
  104.7 5.9 %collective-permute-start.8 = (f32[3,12,128]{2,1,0:T(8,128)}, f32[3,12,128]{2,1,0:T(8,128)S(1)}, u32[]{:S(2)}, u32[]{:S(2)}) collective-permute-start(f32[3,12,128]{2,1,0:T(8,128)} %get-tuple-element.28.s0), channel_id=1, source_target_pairs={{0,384},{128,0},{256,128},{384,256},{1,385},{129,1},{257,129},{385... | collective-permute-start | bytes 55304 | tf_op jit(solution)/shard_map/ppermute | solution.py:243
  108.6 2.0 %copy-start.12 = (f32[3,12,128]{2,1,0:T(8,128)}, f32[3,12,128]{2,1,0:T(8,128)S(1)}, u32[]{:S(2)}) copy-start(f32[3,12,128]{2,1,0:T(8,128)S(1)} %collective-permute-done.6.s1) | copy-start | bytes 55300
  110.3 0.6 copy-start.13
  114.8 24.9 %collective-permute-start.10 = (bf16[8,64,128]{2,1,0:T(8,128)(2,1)}, bf16[8,64,128]{2,1,0:T(8,128)(2,1)S(1)}, u32[]{:S(2)}, u32[]{:S(2)}) collective-permute-start(bf16[8,64,128]{2,1,0:T(8,128)(2,1)} %get-tuple-element.33), channel_id=1, source_target_pairs={{0,2},{2,34},{4,66},{6,98},{32,4},{34,36},{36,68},{38,100},{64,6},... | collective-permute-start | bytes 393224 | tf_op jit(solution)/shard_map/ppermute | solution.py:257
  124.0 19.6 %collective-permute-start.11 = (bf16[8,64,128]{2,1,0:T(8,128)(2,1)}, bf16[8,64,128]{2,1,0:T(8,128)(2,1)S(1)}, u32[]{:S(2)}, u32[]{:S(2)}) collective-permute-start(bf16[8,64,128]{2,1,0:T(8,128)(2,1)} %get-tuple-element.34), channel_id=1, source_target_pairs={{0,4},{2,36},{4,68},{6,100},{32,6},{34,38},{36,70},{38,102},{64,0}... | collective-permute-start | bytes 393224 | tf_op jit(solution)/shard_map/ppermute | solution.py:257
  125.9 22.4 %collective-permute-start.12 = (bf16[8,64,128]{2,1,0:T(8,128)(2,1)}, bf16[8,64,128]{2,1,0:T(8,128)(2,1)S(1)}, u32[]{:S(2)}, u32[]{:S(2)}) collective-permute-start(bf16[8,64,128]{2,1,0:T(8,128)(2,1)} %get-tuple-element.35), channel_id=1, source_target_pairs={{0,6},{2,38},{4,70},{6,102},{32,0},{34,32},{36,64},{38,96},{64,2},... | collective-permute-start | bytes 393224 | tf_op jit(solution)/shard_map/ppermute | solution.py:257
  129.8 24.3 %collective-permute-start.9 = (bf16[8,64,128]{2,1,0:T(8,128)(2,1)}, bf16[8,64,128]{2,1,0:T(8,128)(2,1)S(1)}, u32[]{:S(2)}, u32[]{:S(2)}) collective-permute-start(bf16[8,64,128]{2,1,0:T(8,128)(2,1)} %get-tuple-element.32), channel_id=1, source_target_pairs={{0,0},{2,32},{4,64},{6,96},{32,2},{34,34},{36,66},{38,98},{64,4},{... | collective-permute-start | bytes 393224 | tf_op jit(solution)/shard_map/ppermute | solution.py:257
  154.1 0.7 collective-permute-start.13
  154.8 26.4 %copy-start.1 = (bf16[4,400,384]{2,1,0:T(8,128)(2,1)}, bf16[4,400,384]{2,1,0:T(8,128)(2,1)S(1)}, u32[]{:S(2)}) copy-start(bf16[4,400,384]{2,1,0:T(8,128)(2,1)S(1)} %all-to-all-done.1.loc_ref) | copy-start | bytes 3686404
  176.9 15.8 %all-to-all-start.3 = ((bf16[4,256,384]{2,1,0:T(8,128)(2,1)}), bf16[4,256,384]{2,1,0:T(8,128)(2,1)S(1)}, u32[]{:S(2)}, u32[]{:S(2)}) async-start(bf16[4,256,384]{2,1,0:T(8,128)(2,1)} %get-tuple-element.29), calls=%async_computation.3 | async-start | bytes 1572864 | tf_op jit(solution)/shard_map/all_to_all | solution.py:254
  192.7 0.9 copy-start.3
  (1 other events, 0.6 us)
